TPU v7x, 512 devices: a whole 4x4x16 slice. The times are simulated.
512 devices in a mesh: tiles: 128 (over z, y, core), rep: 4 (over x).
Axes of the slice: x: 4, y: 4, z: 16, core: 2. Of those that a mesh axis runs over, the one named last changes fastest.
Arguments:
- tiles: bfloat16 [1024, 64, 4096], P(('tiles', 'rep')), may hold values from -6 to 6
- block_one: int32 [1024], P(('tiles', 'rep')), may hold values from 0 to 127
- block_two: int32 [1024], P(('tiles', 'rep')), may hold values from 0 to 255
- block_three: int32 [1024], P(('tiles', 'rep')), may hold values from 0 to 15
- owner_map: int32 [128], replicated, may hold values from 0 to 127, each once
- u_one: float32 [32, 8192], P(None, 'tiles'), may hold values from -6 to 6
- u_two: bfloat16 [32, 16384], P(None, 'tiles'), may hold values from -6 to 6
- u_three: bfloat16 [32, 1024], replicated, may hold values from -6 to 6
Outputs:
- factor: float32 [32, 8192], P(None, 'tiles')
- tile_factor: bfloat16 [1024, 2048], P(('tiles', 'rep'))
All inputs are finite; a program needn't handle non-finite values.
Results may differ from a plain program's by a relative error of at most 0.0081.
Values may be sent and summed in bfloat16 or wider, within the bound.
A program may use at most 64 MiB of HBM per device.

v0:
```python
import jax
import jax.numpy as jnp
from jax import lax
from jax.sharding import PartitionSpec as P

NS_STEPS = 2


def pick(table, index, width):
    grid = table.reshape(table.shape[0], -1, width)
    return jnp.transpose(jnp.take(grid, index, axis=1), (1, 0, 2))


def gram_total(local):
    return lax.psum(local, "tiles")


def orthonormal(rows, rows_total):
    hi = lax.Precision.HIGHEST
    rank = rows.shape[0]
    g0 = gram_total(jnp.dot(rows, rows.T, precision=hi, preferred_element_type=jnp.float32))
    msq = jnp.trace(g0) / rows_total
    inv = 1.0 / jnp.sqrt(msq + 1e-06)
    x = rows * inv
    g = g0 * (inv * inv) / rows_total
    eye = jnp.eye(rank, dtype=jnp.float32)
    for step in range(NS_STEPS):
        if step > 0:
            g = (
                gram_total(jnp.dot(x, x.T, precision=hi, preferred_element_type=jnp.float32))
                / rows_total
            )
        x = jnp.dot(1.5 * eye - 0.5 * g, x, precision=hi, preferred_element_type=jnp.float32)
    return x


def spread(current):
    cast = current.astype(jnp.bfloat16)
    return lax.all_gather(cast, "tiles", axis=1, tiled=True)


def per_device(tiles, block_one, block_two, block_three, owner_map, u_one, u_two, u_three):
    hi = lax.Precision.HIGHEST
    count = tiles.shape[0]
    width = tiles.shape[1]
    rank = u_three.shape[0]
    blocks_total = owner_map.shape[0]
    rows_total = blocks_total * width
    two_full = lax.all_gather(u_two, "tiles", axis=1, tiled=True)
    two_pick = pick(two_full, block_two, width)
    three_pick = pick(u_three, block_three, width)
    cube = tiles.reshape(count, width, width, width)
    first = jnp.einsum(
        "tijk,tsk->tijs", cube, three_pick, preferred_element_type=jnp.float32
    ).astype(jnp.bfloat16)
    second = jnp.einsum("tijs,trj->tirs", first, two_pick, preferred_element_type=jnp.float32)
    products = second.reshape(count, width, rank * rank).astype(jnp.bfloat16)
    positions = jnp.take(owner_map, block_one)
    onehot = (positions[:, None] == jnp.arange(blocks_total, dtype=jnp.int32)[None, :]).astype(
        jnp.float32
    )
    current = u_one
    readers = pick(spread(current), positions, width)
    partial_value = jnp.einsum("tic,tri->rc", products, readers, preferred_element_type=jnp.float32)
    project = lax.psum(partial_value, ("tiles", "rep")).astype(jnp.bfloat16)
    z_tile = jnp.einsum("rc,tic->tri", project, products, preferred_element_type=jnp.float32)
    term = jnp.einsum("tri,tn->rni", z_tile, onehot, precision=hi).reshape(rank, rows_total)
    rows = lax.psum_scatter(term, "tiles", scatter_dimension=1, tiled=True)
    rows = lax.psum(rows, "rep")
    current = orthonormal(rows, rows_total)
    tile_factor = pick(spread(current), positions, width).reshape(count, rank * width)
    return (current, tile_factor)


def solution(mesh):
    in_specs = (
        P(("tiles", "rep"), None, None),
        P(("tiles", "rep")),
        P(("tiles", "rep")),
        P(("tiles", "rep")),
        P(),
        P(None, "tiles"),
        P(None, "tiles"),
        P(),
    )
    out_specs = (P(None, "tiles"), P(("tiles", "rep"), None))
    return jax.shard_map(
        per_device, mesh=mesh, in_specs=in_specs, out_specs=out_specs, check_vma=False
    )
```

profile of v0, /device:TPU:1, one launch (start us, length us, event | category | flops | bytes accessed | tf_op | source)
XLA Modules:
  0.0 1633.5 jit_solution(5011610970250502089)
XLA Ops:
  8.6 0.7 convert_bitcast_fusion.1
  9.3 1.0 reshape.51
  10.4 109.1 %all-gather = bf16[128,64,32]{1,2,0:T(8,128)(2,1)S(1)} all-gather(bf16[1,64,32]{1,2,0:T(8,128)(2,1)S(1)} %convert_bitcast_fusion.1), channel_id=1, replica_groups=mesh['tiles'=128,'rep'=4] {'tiles'}, dimensions={0}, use_global_device_ids=true | all-gather | bytes 528384 | tf_op jit(solution)/shard_map/all_gather | solution.py:39
  119.9 0.8 reshape.103
  120.7 1.1 reshape.53
  122.6 3.4 reshape.52
  128.0 2.0 fusion
  130.0 17.5 %all-gather.4.cloned.1.call-done = bf16[32,16384]{1,0:T(8,128)(2,1)} async-done(((bf16[32,128]{1,0:T(8,128)(2,1)}), bf16[32,16384]{1,0:T(8,128)(2,1)}) %all-gather.4.cloned.1.call-update) | async-done | bytes 1048592 | tf_op jit(solution)/shard_map/all_gather | solution.py:49
  147.5 3.0 reshape.50
  150.6 2.7 copy.27
  153.3 2.1 gather_fusion.1
  155.4 1.1 fusion.1
  157.0 102.8 %all-reduce.1 = bf16[32,1024]{1,0:T(8,128)(2,1)S(1)} all-reduce(f32[32,1024]{1,0:T(8,128)S(1)} %convolution_bitcast_fusion.1), channel_id=1, replica_groups=mesh['tiles'=128,'rep'=4] {'tiles','rep'}, use_global_device_ids=true, to_apply=%region_0.0 | all-reduce | flops 32768 | bytes 196608 | tf_op jit(solution)/shard_map/psum | solution.py:65
  259.9 1.0 convolution_bitcast_fusion
  261.0 4.4 copy.45
  265.5 245.9 %reduce-scatter.4.cloned.1.call-done = f32[64,32]{1,0:T(8,128)} async-done(((f32[8192,32]{1,0:T(8,128)}), f32[64,32]{1,0:T(8,128)}) %reduce-scatter.4.cloned.1.call-update) | async-done | bytes 8208
  511.3 0.8 copy.44
  512.2 13.3 psum.29
  525.6 500.6 %psum.30 = f32[32,32]{1,0:T(8,128)S(1)} all-reduce(f32[32,32]{1,0:T(8,128)S(1)} %fusion.44), channel_id=1, replica_groups=mesh['tiles'=128,'rep'=4] {'tiles'}, use_global_device_ids=true, to_apply=%region_3.5 | all-reduce | flops 1024 | bytes 8192 | tf_op jit(solution)/shard_map/psum | solution.py:15
  1027.9 490.9 %psum.31 = f32[32,32]{1,0:T(8,128)S(1)} all-reduce(f32[32,32]{1,0:T(8,128)S(1)} %fusion.45), channel_id=1, replica_groups=mesh['tiles'=128,'rep'=4] {'tiles'}, use_global_device_ids=true, to_apply=%region_5.7 | all-reduce | flops 1024 | bytes 8192 | tf_op jit(solution)/shard_map/psum | solution.py:15
  1518.9 103.3 %all-gather.1 = bf16[128,64,32]{1,2,0:T(8,128)(2,1)S(1)} all-gather(bf16[1,64,32]{1,2,0:T(8,128)(2,1)S(1)} %convert_bitcast_fusion), channel_id=1, replica_groups=mesh['tiles'=128,'rep'=4] {'tiles'}, dimensions={0}, use_global_device_ids=true | all-gather | bytes 528384 | tf_op jit(solution)/shard_map/all_gather | solution.py:39
  1622.6 0.8 reshape.105
  1623.5 1.1 reshape.55
  1625.9 0.7 reshape.56
  (44 shorter events, 8.0 us)
Async XLA Ops:
  7.2 118.9 %copy-start = (s32[128]{0:T(128)S(1)}, s32[128]{0:T(128)}, u32[]{:S(2)}) copy-start(s32[128]{0:T(128)} %param.14) | copy-start | bytes 1540
  7.2 140.3 %all-gather.4.cloned.1.call-start = ((), (), s32[]{:S(2)}) async-start(), calls=%async_computation.1 | async-start | bytes 1056768 | tf_op jit(solution)/shard_map/all_gather | solution.py:49
  7.9 503.4 %reduce-scatter.4.cloned.1.call-start = ((), (), s32[]{:S(2)}) async-start(), calls=%async_computation.2 | async-start | bytes 4227072
  122.6 4.2 copy-start.4
  122.6 4.7 copy-start.2
  122.6 5.3 copy-start.3
  1518.9 104.6 %copy-start.1 = (f32[32,64]{1,0:T(8,128)}, f32[32,64]{1,0:T(8,128)S(1)}, u32[]{:S(2)}) copy-start(f32[32,64]{1,0:T(8,128)S(1)} %fusion.7) | copy-start | bytes 24580
Sparse Core Ops, SparseCore 0:
  11.0 136.4 all-gather.3
  265.6 245.7 reduce-scatter.3
where the time goes:
time: 1630 us
  blocking collectives  1320 us (81%)
  waiting for transfers between devices  264 us (16%)
  local copies, waits for them, and re-layouts  27 us (2%)
    psum x2, blocking collectives, gram_total(): return lax.psum(local, 'tiles')  992 us
    unnamed x3, waiting for transfers between devices  247 us
    all_gather x2, blocking collectives, spread(): return lax.all_gather(cast, 'tiles', axis=1, tiled=True)  212 us
    psum x1, blocking collectives, per_device(): project = lax.psum(partial_value, ('tiles', 'rep')).astype(jnp.bfloat16)  103 us
  transfers between devices with their start and end apart: 2, of which 2 were waited for; matrix products, arithmetic and copies ran while one was open for 1% of the time, Pallas kernels for 0%

commit v1 on v0

--- a/solution.py
+++ b/solution.py
@@ -62,7 +62,7 @@
     current = u_one
     readers = pick(spread(current), positions, width)
     partial_value = jnp.einsum("tic,tri->rc", products, readers, preferred_element_type=jnp.float32)
-    project = lax.psum(partial_value, ("tiles", "rep")).astype(jnp.bfloat16)
+    project = lax.psum(lax.psum(partial_value, "rep"), "tiles").astype(jnp.bfloat16)
     z_tile = jnp.einsum("rc,tic->tri", project, products, preferred_element_type=jnp.float32)
     term = jnp.einsum("tri,tn->rni", z_tile, onehot, precision=hi).reshape(rank, rows_total)
     rows = lax.psum_scatter(term, "tiles", scatter_dimension=1, tiled=True)

time: 1630 us -> 2080 us (1.28)
  blocking collectives: 1320 us -> 1710 us
  waiting for transfers between devices: 264 us -> 322 us
    psum x1, blocking collectives: 103 us -> 491 us  [per_device(): lax.psum(lax.psum(partial_value, 'rep'), 'tiles').astype(jnp.bfloat16)]
    psum x0 -> x1, waiting for transfers between devices: none -> 49.8 us  [per_device(): lax.psum(partial_value, 'rep')]
    unnamed x3 -> x4, waiting for transfers between devices: 247 us -> 255 us
  transfers between devices with their start and end apart: 2 -> 3, of which waited for: 2 -> 3; matrix products, arithmetic and copies ran while one was open for 1% -> 1% of each run, Pallas kernels for 0% -> 0%
where the time goes in v1:
time: 2080 us
  blocking collectives  1710 us (82%)
  waiting for transfers between devices  322 us (15%)
  local copies, waits for them, and re-layouts  27 us (1%)
    psum x2, blocking collectives, gram_total(): return lax.psum(local, 'tiles')  991 us
    psum x1, blocking collectives, per_device(): lax.psum(lax.psum(partial_value, 'rep'), 'tiles').astype(jnp.bfloat16)  491 us
    unnamed x4, waiting for transfers between devices  255 us
    all_gather x2, blocking collectives, spread(): return lax.all_gather(cast, 'tiles', axis=1, tiled=True)  212 us
    psum x1, waiting for transfers between devices, per_device(): lax.psum(partial_value, 'rep')  49.8 us
  transfers between devices with their start and end apart: 3, of which 3 were waited for; matrix products, arithmetic and copies ran while one was open for 1% of the time, Pallas kernels for 0%

profile of v1, /device:TPU:1, one launch (start us, length us, event | category | flops | bytes accessed | tf_op | source)
XLA Modules:
  0.0 2080.5 jit_solution(5322688300808266680)
XLA Ops:
  9.3 1.0 reshape.51
  10.4 109.1 %all-gather = bf16[128,64,32]{1,2,0:T(8,128)(2,1)S(1)} all-gather(bf16[1,64,32]{1,2,0:T(8,128)(2,1)S(1)} %convert_bitcast_fusion.1), channel_id=1, replica_groups=mesh['tiles'=128,'rep'=4] {'tiles'}, dimensions={0}, use_global_device_ids=true | all-gather | bytes 528384 | tf_op jit(solution)/shard_map/all_gather | solution.py:39
  119.9 0.8 reshape.103
  120.7 1.1 reshape.53
  122.6 3.4 reshape.52
  128.0 2.0 fusion
  130.0 17.5 all-gather.4.cloned.1.call-done
  147.5 3.0 reshape.50
  150.6 2.7 copy.27
  153.3 2.1 gather_fusion.1
  155.4 1.1 fusion.1
  156.7 0.9 convolution_bitcast_fusion.1
  157.7 49.8 %all-reduce.3.cloned.1.call-done = f32[32,1024]{1,0:T(8,128)} async-done(((f32[32,1024]{1,0:T(8,128)}), f32[32,1024]{1,0:T(8,128)}) %all-reduce.3.cloned.1.call-update) | async-done | bytes 131088 | tf_op jit(solution)/shard_map/psum | solution.py:65
  207.5 491.5 %all-reduce.4 = bf16[32,1024]{1,0:T(8,128)(2,1)S(1)} all-reduce(f32[32,1024]{1,0:T(8,128)} %all-reduce.3.cloned.1.call-done), channel_id=1, replica_groups=mesh['tiles'=128,'rep'=4] {'tiles'}, use_global_device_ids=true, to_apply=%region_1.3 | all-reduce | flops 32768 | bytes 196608 | tf_op jit(solution)/shard_map/psum | solution.py:65
  699.2 1.0 convolution_bitcast_fusion
  700.3 4.4 copy.45
  704.7 253.9 %reduce-scatter.4.cloned.1.call-done = f32[64,32]{1,0:T(8,128)} async-done(((f32[8192,32]{1,0:T(8,128)}), f32[64,32]{1,0:T(8,128)}) %reduce-scatter.4.cloned.1.call-update) | async-done | bytes 8208
  958.7 0.8 copy.44
  959.5 13.4 psum.37
  973.0 500.6 %psum.38 = f32[32,32]{1,0:T(8,128)S(1)} all-reduce(f32[32,32]{1,0:T(8,128)S(1)} %fusion.44), channel_id=1, replica_groups=mesh['tiles'=128,'rep'=4] {'tiles'}, use_global_device_ids=true, to_apply=%region_4.6 | all-reduce | flops 1024 | bytes 8192 | tf_op jit(solution)/shard_map/psum | solution.py:15
  1475.2 490.9 %psum.39 = f32[32,32]{1,0:T(8,128)S(1)} all-reduce(f32[32,32]{1,0:T(8,128)S(1)} %fusion.45), channel_id=1, replica_groups=mesh['tiles'=128,'rep'=4] {'tiles'}, use_global_device_ids=true, to_apply=%region_6.8 | all-reduce | flops 1024 | bytes 8192 | tf_op jit(solution)/shard_map/psum | solution.py:15
  1966.3 103.3 %all-gather.1 = bf16[128,64,32]{1,2,0:T(8,128)(2,1)S(1)} all-gather(bf16[1,64,32]{1,2,0:T(8,128)(2,1)S(1)} %convert_bitcast_fusion), channel_id=1, replica_groups=mesh['tiles'=128,'rep'=4] {'tiles'}, dimensions={0}, use_global_device_ids=true | all-gather | bytes 528384 | tf_op jit(solution)/shard_map/all_gather | solution.py:39
  2070.0 0.8 reshape.105
  2070.8 1.1 reshape.55
  (47 shorter events, 9.2 us)
Async XLA Ops:
  7.2 118.9 %copy-start = (s32[128]{0:T(128)S(1)}, s32[128]{0:T(128)}, u32[]{:S(2)}) copy-start(s32[128]{0:T(128)} %param.14) | copy-start | bytes 1540
  7.2 140.3 %all-gather.4.cloned.1.call-start = ((), (), s32[]{:S(2)}) async-start(), calls=%async_computation.1 | async-start | bytes 1056768 | tf_op jit(solution)/shard_map/all_gather | solution.py:49
  7.9 199.6 %all-reduce.3.cloned.1.call-start = ((), (), s32[]{:S(2)}) async-start(), calls=%async_computation.2 | async-start | bytes 262144 | tf_op jit(solution)/shard_map/psum | solution.py:65
  122.6 4.2 copy-start.4
  122.6 4.7 copy-start.2
  122.6 5.3 copy-start.3
  157.7 801.0 %reduce-scatter.4.cloned.1.call-start = ((), (), s32[]{:S(2)}) async-start(), calls=%async_computation.3 | async-start | bytes 4227072
  1966.2 104.6 %copy-start.1 = (f32[32,64]{1,0:T(8,128)}, f32[32,64]{1,0:T(8,128)S(1)}, u32[]{:S(2)}) copy-start(f32[32,64]{1,0:T(8,128)S(1)} %fusion.7) | copy-start | bytes 24580
Sparse Core Ops, SparseCore 0:
  11.0 136.4 all-gather.3
  157.8 49.6 all-reduce.2
  704.9 253.7 reduce-scatter.3

commit v2 on v0

--- a/solution.py
+++ b/solution.py
@@ -36,7 +36,9 @@
 
 def spread(current):
     cast = current.astype(jnp.bfloat16)
-    return lax.all_gather(cast, "tiles", axis=1, tiled=True)
+    return jnp.concatenate(
+        lax.all_to_all(jnp.stack([cast] * lax.axis_size("tiles")), "tiles", 0, 0), axis=1
+    )
 
 
 def per_device(tiles, block_one, block_two, block_three, owner_map, u_one, u_two, u_three):

time: 1630 us -> 1580 us (0.969)
  blocking collectives: 1320 us -> 1160 us
  waiting for transfers between devices: 264 us -> 359 us
  starting transfers between devices: 0.08 us -> 21.1 us
    all_gather x2 -> x0, blocking collectives: 212 us -> none  [spread(): return lax.all_gather(cast, 'tiles', axis=1, tiled=True)]
    all_gather x1, waiting for transfers between devices: 17.5 us -> 113 us  [per_device(): two_full = lax.all_gather(u_two, 'tiles', axis=1, tiled=True)]
    all_to_all x0 -> x1, blocking collectives: none -> 47.5 us  [spread(): lax.all_to_all(jnp.stack([cast] * lax.axis_size('tiles')), 'tiles', 0, 0)]
    all_to_all x0 -> x1, starting transfers between devices: none -> 21 us  [spread(): lax.all_to_all(jnp.stack([cast] * lax.axis_size('tiles')), 'tiles', 0, 0)]
  transfers between devices with their start and end apart: 2 -> 3, of which waited for: 2 -> 2; matrix products, arithmetic and copies ran while one was open for 1% -> 1% of each run, Pallas kernels for 0% -> 0%
where the time goes in v2:
time: 1580 us
  blocking collectives  1160 us (73%)
  waiting for transfers between devices  359 us (23%)
  local copies, waits for them, and re-layouts  24.1 us (2%)
  starting transfers between devices  21.1 us (1%)
    psum x2, blocking collectives, gram_total(): return lax.psum(local, 'tiles')  991 us
    unnamed x3, waiting for transfers between devices  246 us
    all_gather x1, waiting for transfers between devices, per_device(): two_full = lax.all_gather(u_two, 'tiles', axis=1, tiled=True)  113 us
    psum x1, blocking collectives, per_device(): project = lax.psum(partial_value, ('tiles', 'rep')).astype(jnp.bfloat16)  103 us
    all_to_all x1, blocking collectives, spread(): lax.all_to_all(jnp.stack([cast] * lax.axis_size('tiles')), 'tiles', 0, 0)  47.5 us
  transfers between devices with their start and end apart: 3, of which 2 were waited for; matrix products, arithmetic and copies ran while one was open for 1% of the time, Pallas kernels for 0%

profile of v2, /device:TPU:1, one launch (start us, length us, event | category | flops | bytes accessed | tf_op | source)
XLA Modules:
  0.0 1581.6 jit_solution(9080636432979419780)
XLA Ops:
  7.3 0.7 all-gather.2.cloned.1.call-update
  8.0 0.7 convert_element_type.31
  8.8 1.4 reshape.117
  10.2 21.0 %all-to-all-start = ((bf16[128,2,1024]{2,1,0:T(2,128)(2,1)}), bf16[128,2,1024]{2,1,0:T(2,128)(2,1)}, u32[]{:S(2)}, u32[]{:S(2)}) async-start(bf16[128,2,1024]{2,1,0:T(2,128)(2,1)} %reshape.117), calls=%async_computation | async-start | bytes 1048576 | tf_op jit(solution)/shard_map/all_to_all | solution.py:40
  31.6 2.3 reshape.56
  33.9 0.6 gather_fusion
  35.2 2.0 fusion
  37.3 112.8 %all-gather.2.cloned.1.call-done = bf16[32,16384]{1,0:T(8,128)(2,1)} async-done(((bf16[32,128]{1,0:T(8,128)(2,1)}), bf16[32,16384]{1,0:T(8,128)(2,1)}) %all-gather.2.cloned.1.call-update) | async-done | bytes 1048592 | tf_op jit(solution)/shard_map/all_gather | solution.py:51
  150.1 3.0 reshape.54
  153.1 2.7 copy.21
  155.8 2.1 gather_fusion.1
  158.0 1.1 fusion.1
  159.3 2.3 reshape.118
  162.3 102.8 %all-reduce.1 = bf16[32,1024]{1,0:T(8,128)(2,1)S(1)} all-reduce(f32[32,1024]{1,0:T(8,128)S(1)} %convolution_bitcast_fusion.1), channel_id=1, replica_groups=mesh['tiles'=128,'rep'=4] {'tiles','rep'}, use_global_device_ids=true, to_apply=%region_0.0 | all-reduce | flops 32768 | bytes 196608 | tf_op jit(solution)/shard_map/psum | solution.py:67
  265.4 1.0 convolution_bitcast_fusion
  266.4 4.4 copy.35
  270.9 245.6 %reduce-scatter.4.cloned.1.call-done = f32[64,32]{1,0:T(8,128)} async-done(((f32[8192,32]{1,0:T(8,128)}), f32[64,32]{1,0:T(8,128)}) %reduce-scatter.4.cloned.1.call-update) | async-done | bytes 8208
  516.5 0.8 copy.34
  517.3 13.3 psum.29
  530.7 500.6 %psum.30 = f32[32,32]{1,0:T(8,128)S(1)} all-reduce(f32[32,32]{1,0:T(8,128)S(1)} %fusion.45), channel_id=1, replica_groups=mesh['tiles'=128,'rep'=4] {'tiles'}, use_global_device_ids=true, to_apply=%region_3.5 | all-reduce | flops 1024 | bytes 8192 | tf_op jit(solution)/shard_map/psum | solution.py:15
  1032.9 490.9 %psum.31 = f32[32,32]{1,0:T(8,128)S(1)} all-reduce(f32[32,32]{1,0:T(8,128)S(1)} %fusion.46), channel_id=1, replica_groups=mesh['tiles'=128,'rep'=4] {'tiles'}, use_global_device_ids=true, to_apply=%region_5.7 | all-reduce | flops 1024 | bytes 8192 | tf_op jit(solution)/shard_map/psum | solution.py:15
  1523.8 0.7 fusion.44
  1525.3 47.5 %all_to_all.10 = bf16[128,2,1024]{2,1,0:T(2,128)(2,1)S(1)} all-to-all(bf16[128,2,1024]{2,1,0:T(2,128)(2,1)S(1)} %reshape.119), channel_id=1, replica_groups=mesh['tiles'=128,'rep'=4] {'tiles'}, dimensions={0} | all-to-all | bytes 1048576 | tf_op jit(solution)/shard_map/all_to_all | solution.py:40
  1574.0 0.7 reshape.60
  (44 shorter events, 5.3 us)
Async XLA Ops:
  7.2 26.7 %copy-start = (s32[128]{0:T(128)S(1)}, s32[128]{0:T(128)}, u32[]{:S(2)}) copy-start(s32[128]{0:T(128)} %param.14) | copy-start | bytes 1540
  7.2 24.2 %copy-start.3 = (s32[2]{0:T(128)S(1)}, s32[2]{0:T(128)}, u32[]{:S(2)}) copy-start(s32[2]{0:T(128)} %param.11) | copy-start | bytes 28
  7.2 24.2 %copy-start.5 = (s32[2]{0:T(128)S(1)}, s32[2]{0:T(128)}, u32[]{:S(2)}) copy-start(s32[2]{0:T(128)} %param.13) | copy-start | bytes 28
  7.2 24.2 %copy-start.2 = (bf16[32,1024]{1,0:T(8,128)(2,1)S(1)}, bf16[32,1024]{1,0:T(8,128)(2,1)}, u32[]{:S(2)}) copy-start(bf16[32,1024]{1,0:T(8,128)(2,1)} %param.17) | copy-start | bytes 196612
  7.2 24.4 %copy-start.1 = (bf16[2,64,4096]{2,1,0:T(8,128)(2,1)S(1)}, bf16[2,64,4096]{2,1,0:T(8,128)(2,1)}, u32[]{:S(2)}) copy-start(bf16[2,64,4096]{2,1,0:T(8,128)(2,1)} %param.10) | copy-start | bytes 3145732
  7.2 142.8 %all-gather.2.cloned.1.call-start = ((), (), s32[]{:S(2)}) async-start(), calls=%async_computation.3 | async-start | bytes 1056768 | tf_op jit(solution)/shard_map/all_gather | solution.py:51
  10.2 149.0 %all-to-all-start = ((bf16[128,2,1024]{2,1,0:T(2,128)(2,1)}), bf16[128,2,1024]{2,1,0:T(2,128)(2,1)}, u32[]{:S(2)}, u32[]{:S(2)}) async-start(bf16[128,2,1024]{2,1,0:T(2,128)(2,1)} %reshape.117), calls=%async_computation | async-start | bytes 1048576 | tf_op jit(solution)/shard_map/all_to_all | solution.py:40
  31.3 3.8 copy-start.4
  31.3 485.2 %reduce-scatter.4.cloned.1.call-start = ((), (), s32[]{:S(2)}) async-start(), calls=%async_computation.4 | async-start | bytes 4227072
Sparse Core Ops, SparseCore 0:
  11.1 138.9 all-gather.1
  271.0 245.4 reduce-scatter.3

commit v3 on v0

--- a/solution.py
+++ b/solution.py
@@ -12,7 +12,7 @@
 
 
 def gram_total(local):
-    return lax.psum(local, "tiles")
+    return jnp.sum(lax.all_gather(local, "tiles"), axis=0)
 
 
 def orthonormal(rows, rows_total):

time: 1630 us -> 854 us (0.52)
  blocking collectives: 1320 us -> 540 us
    psum x2 -> x0, blocking collectives: 992 us -> none  [gram_total(): return lax.psum(local, 'tiles')]
    all_gather x0 -> x2, blocking collectives: none -> 215 us  [gram_total(): return jnp.sum(lax.all_gather(local, 'tiles'), axis=0)]
where the time goes in v3:
time: 854 us
  blocking collectives  540 us (63%)
  waiting for transfers between devices  264 us (31%)
  local copies, waits for them, and re-layouts  27 us (3%)
  between operations  15 us (2%)
    unnamed x3, waiting for transfers between devices  247 us
    all_gather x2, blocking collectives, gram_total(): return jnp.sum(lax.all_gather(local, 'tiles'), axis=0)  215 us
    all_gather x2, blocking collectives, spread(): return lax.all_gather(cast, 'tiles', axis=1, tiled=True)  209 us
    psum x1, blocking collectives, per_device(): project = lax.psum(partial_value, ('tiles', 'rep')).astype(jnp.bfloat16)  103 us
    all_gather x1, waiting for transfers between devices, per_device(): two_full = lax.all_gather(u_two, 'tiles', axis=1, tiled=True)  17.5 us
  transfers between devices with their start and end apart: 2, of which 2 were waited for; matrix products, arithmetic and copies ran while one was open for 1% of the time, Pallas kernels for 0%

profile of v3, /device:TPU:1, one launch (start us, length us, event | category | flops | bytes accessed | tf_op | source)
XLA Modules:
  0.0 853.6 jit_solution(17320908478926892155)
XLA Ops:
  8.6 0.7 convert_bitcast_fusion.1
  9.3 1.0 reshape.51
  10.4 109.1 %all-gather.2 = bf16[128,64,32]{1,2,0:T(8,128)(2,1)S(1)} all-gather(bf16[1,64,32]{1,2,0:T(8,128)(2,1)S(1)} %convert_bitcast_fusion.1), channel_id=1, replica_groups=mesh['tiles'=128,'rep'=4] {'tiles'}, dimensions={0}, use_global_device_ids=true | all-gather | bytes 528384 | tf_op jit(solution)/shard_map/all_gather | solution.py:39
  119.9 0.8 reshape.105
  120.7 1.1 reshape.53
  122.6 3.4 reshape.52
  128.0 2.0 fusion
  130.0 17.5 %all-gather.6.cloned.1.call-done = bf16[32,16384]{1,0:T(8,128)(2,1)} async-done(((bf16[32,128]{1,0:T(8,128)(2,1)}), bf16[32,16384]{1,0:T(8,128)(2,1)}) %all-gather.6.cloned.1.call-update) | async-done | bytes 1048592 | tf_op jit(solution)/shard_map/all_gather | solution.py:49
  147.5 3.0 reshape.50
  150.6 2.7 copy.39
  153.3 2.1 gather_fusion.1
  155.4 1.1 fusion.1
  157.0 102.8 %all-reduce.1 = bf16[32,1024]{1,0:T(8,128)(2,1)S(1)} all-reduce(f32[32,1024]{1,0:T(8,128)S(1)} %convolution_bitcast_fusion.1), channel_id=1, replica_groups=mesh['tiles'=128,'rep'=4] {'tiles','rep'}, use_global_device_ids=true, to_apply=%region_0.0 | all-reduce | flops 32768 | bytes 196608 | tf_op jit(solution)/shard_map/psum | solution.py:65
  259.9 1.0 convolution_bitcast_fusion
  261.0 4.4 copy.57
  265.5 245.9 %reduce-scatter.4.cloned.1.call-done = f32[64,32]{1,0:T(8,128)} async-done(((f32[8192,32]{1,0:T(8,128)}), f32[64,32]{1,0:T(8,128)}) %reduce-scatter.4.cloned.1.call-update) | async-done | bytes 8208
  511.3 0.8 copy.56
  512.2 13.3 %psum.15 = f32[32,64]{1,0:T(8,128)S(1)} all-reduce(f32[32,64]{1,0:T(8,128)S(1)} %copy.56), channel_id=1, replica_groups=mesh['tiles'=128,'rep'=4] {'rep'}, use_global_device_ids=true, to_apply=%region_2.4 | all-reduce | flops 2048 | bytes 16384 | tf_op jit(solution)/shard_map/psum | solution.py:69
  525.6 115.5 %all-gather = f32[4096,32]{1,0:T(8,128)S(1)} all-gather(f32[32,32]{1,0:T(8,128)S(1)} %fusion.44), channel_id=2, replica_groups=mesh['tiles'=128,'rep'=4] {'tiles'}, dimensions={0}, use_global_device_ids=true | all-gather | bytes 528384 | tf_op jit(solution)/shard_map/all_gather | solution.py:15
  642.9 99.5 %all-gather.1 = f32[4096,32]{1,0:T(8,128)S(1)} all-gather(f32[32,32]{1,0:T(8,128)S(1)} %fusion.45), channel_id=3, replica_groups=mesh['tiles'=128,'rep'=4] {'tiles'}, dimensions={0}, use_global_device_ids=true | all-gather | bytes 528384 | tf_op jit(solution)/shard_map/all_gather | solution.py:15
  742.7 99.6 %all-gather.3 = bf16[128,64,32]{1,2,0:T(8,128)(2,1)S(1)} all-gather(bf16[1,64,32]{1,2,0:T(8,128)(2,1)S(1)} %convert_bitcast_fusion), channel_id=1, replica_groups=mesh['tiles'=128,'rep'=4] {'tiles'}, dimensions={0}, use_global_device_ids=true | all-gather | bytes 528384 | tf_op jit(solution)/shard_map/all_gather | solution.py:39
  842.8 0.8 reshape.107
  843.6 1.1 reshape.55
  846.1 0.7 reshape.56
  (46 shorter events, 8.4 us)
Async XLA Ops:
  7.2 118.9 %copy-start = (s32[128]{0:T(128)S(1)}, s32[128]{0:T(128)}, u32[]{:S(2)}) copy-start(s32[128]{0:T(128)} %param.14) | copy-start | bytes 1540
  7.2 140.3 %all-gather.6.cloned.1.call-start = ((), (), s32[]{:S(2)}) async-start(), calls=%async_computation.1 | async-start | bytes 1056768 | tf_op jit(solution)/shard_map/all_gather | solution.py:49
  7.9 503.4 %reduce-scatter.4.cloned.1.call-start = ((), (), s32[]{:S(2)}) async-start(), calls=%async_computation.2 | async-start | bytes 4227072
  122.6 4.2 copy-start.4
  122.6 4.7 copy-start.2
  122.6 5.3 copy-start.3
  742.7 100.9 %copy-start.1 = (f32[32,64]{1,0:T(8,128)}, f32[32,64]{1,0:T(8,128)S(1)}, u32[]{:S(2)}) copy-start(f32[32,64]{1,0:T(8,128)S(1)} %fusion.7) | copy-start | bytes 24580
Sparse Core Ops, SparseCore 0:
  11.0 136.4 all-gather.5
  265.6 245.7 reduce-scatter.3
